TPU v7x, 32 devices: a whole 2x2x4 slice. The times are simulated.
32 devices in a mesh: gx: 2 (over y), gy: 4 (over z), gz: 4 (over x, core).
Axes of the slice: x: 2, y: 2, z: 4, core: 2. Of those that a mesh axis runs over, the one named last changes fastest.
Arguments:
- load_cases: float32 [2, 128, 32, 256], P(None, 'gz', 'gy', 'gx'), may hold values from -6 to 6
- density_level: int32 [128, 32, 256], P('gz', 'gy', 'gx'), may hold values from 0 to 7
Outputs:
- solution: float32 [2, 128, 32, 256], P(None, 'gz', 'gy', 'gx')
All inputs are finite; a program needn't handle non-finite values.
Results may differ from a plain program's by a relative error of at most 0.00011.
Values sent between devices are 32-bit elements; how exact they have to be, the bound alone decides.
A program may use at most 192 MiB of HBM per device.

v0:
```python
import math

import jax
import jax.numpy as jnp
from jax import lax
from jax.sharding import PartitionSpec as P

LEVELS = 8


middle_point = 0.646875
half_range = 0.503125
first_weight = 1.0 / (middle_point + half_range * math.cos(math.pi / 4))
second_weight = 1.0 / (middle_point - half_range * math.cos(math.pi / 4))


def with_halo(cells, sides, width):
    for axis, dim in sides:
        count = lax.axis_size(axis)
        ends = count - 1
        head = lax.slice_in_dim(cells, 0, width, axis=dim)
        tail = lax.slice_in_dim(cells, cells.shape[dim] - width, cells.shape[dim], axis=dim)
        cells = jnp.concatenate(
            [
                lax.ppermute(tail, axis, [(i, (i + 1) % count) for i in range(ends)]),
                cells,
                lax.ppermute(head, axis, [((i + 1) % count, i) for i in range(ends)]),
            ],
            axis=dim,
        )
    return cells


def smooth_sum(padded):
    padded = 0.5 * padded[:, :-2] + padded[:, 1:-1] + 0.5 * padded[:, 2:]
    padded = 0.5 * padded[:, :, :-2] + padded[:, :, 1:-1] + 0.5 * padded[:, :, 2:]
    return 0.5 * padded[..., :-2] + padded[..., 1:-1] + 0.5 * padded[..., 2:]


def operate_fine(values, stiffness, spacing_sq):
    padded = with_halo(values, (("gx", 3), ("gy", 2), ("gz", 1)), 1)
    return stiffness * (16.0 * values - 2.0 * smooth_sum(padded)) / spacing_sq


def operate_joined(values, stiffness, spacing_sq):
    padded = with_halo(values, (("gy", 2), ("gz", 1)), 1)
    padded = jnp.pad(padded, ((0, 0), (0, 0), (0, 0), (1, 1)))
    return stiffness * (16.0 * values - 2.0 * smooth_sum(padded)) / spacing_sq


def jacobi(residue, stiffness, spacing_sq):
    return residue * (spacing_sq / (14.0 * stiffness))


def restrict(values):
    return values.reshape(
        values.shape[0], values.shape[1] // 2, 2, values.shape[2] // 2, 2, values.shape[3] // 2, 2
    ).mean(axis=(2, 4, 6))


def prolong(values):
    return jnp.repeat(jnp.repeat(jnp.repeat(values, 2, axis=1), 2, axis=2), 2, axis=3)


def presmooth(target, stiffness, spacing_sq, operator):
    guess = first_weight * jacobi(target, stiffness, spacing_sq)
    return guess + second_weight * jacobi(
        target - operator(guess, stiffness, spacing_sq), stiffness, spacing_sq
    )


def postsmooth(guess, target, stiffness, spacing_sq, operator):
    guess = guess + first_weight * jacobi(
        target - operator(guess, stiffness, spacing_sq), stiffness, spacing_sq
    )
    return guess + second_weight * jacobi(
        target - operator(guess, stiffness, spacing_sq), stiffness, spacing_sq
    )


def coarse_cycle(rhs_joined, stiffness_joined, operator):
    guess_joined = presmooth(rhs_joined, stiffness_joined, 16.0, operator)
    rhs_base = restrict(rhs_joined - operator(guess_joined, stiffness_joined, 16.0))
    stiffness_base = restrict(stiffness_joined)
    guess_base = presmooth(rhs_base, stiffness_base, 64.0, operator)
    guess_base = postsmooth(guess_base, rhs_base, stiffness_base, 64.0, operator)
    return postsmooth(
        guess_joined + prolong(guess_base), rhs_joined, stiffness_joined, 16.0, operator
    )


def coarse_levels(rhs_low, stiffness_low):
    depth_own, width_own, length_own = (rhs_low.shape[1], rhs_low.shape[2], rhs_low.shape[3])
    rhs_joined, stiffness_joined = (
        lax.all_gather(rhs_low, "gx", axis=3, tiled=True),
        lax.all_gather(stiffness_low, "gx", axis=3, tiled=True),
    )
    guess_joined = coarse_cycle(rhs_joined, stiffness_joined, operate_joined)
    return lax.dynamic_slice_in_dim(guess_joined, lax.axis_index("gx") * length_own, length_own, 3)


def body(load_cases, density_level):
    stiffness_fine = (0.05 + 0.95 * (density_level.astype(jnp.float32) / (LEVELS - 1)) ** 3)[None]
    stiffness_mid = restrict(stiffness_fine)
    stiffness_low = restrict(stiffness_mid)
    guess_fine = presmooth(load_cases, stiffness_fine, 1.0, operate_fine)
    rhs_mid = restrict(load_cases - operate_fine(guess_fine, stiffness_fine, 1.0))
    guess_mid = presmooth(rhs_mid, stiffness_mid, 4.0, operate_fine)
    rhs_low = restrict(rhs_mid - operate_fine(guess_mid, stiffness_mid, 4.0))
    guess_low = coarse_levels(rhs_low, stiffness_low)
    guess_mid = postsmooth(
        guess_mid + prolong(guess_low), rhs_mid, stiffness_mid, 4.0, operate_fine
    )
    return postsmooth(
        guess_fine + prolong(guess_mid), load_cases, stiffness_fine, 1.0, operate_fine
    )


def solution(mesh):
    in_specs = (P(None, "gz", "gy", "gx"), P("gz", "gy", "gx"))
    out_specs = P(None, "gz", "gy", "gx")
    return jax.shard_map(body, mesh=mesh, in_specs=in_specs, out_specs=out_specs, check_vma=False)
```

profile of v0, /device:TPU:0, one launch (start us, length us, event | category | flops | bytes accessed | tf_op | source)
XLA Modules:
  0.0 365.1 jit_solution(2103858053409375654)
XLA Ops:
  2.1 4.9 %collective-permute-start = (f32[2,32,8,1]{3,2,1,0:T(8,128)S(1)}, f32[2,32,8,1]{3,2,1,0:T(8,128)S(1)}, u32[]{:S(2)}, u32[]{:S(2)}) collective-permute-start(f32[2,32,8,1]{3,2,1,0:T(8,128)S(1)} %get-tuple-element.31), channel_id=1, source_target_pairs={{0,16},{1,17},{2,18},{3,19},{4,20},{5,21},{6,22},{7,23},{8,24},{9,... | collective-permute-start | bytes 6152 | tf_op jit(solution)/shard_map/ppermute | solution.py:25
  8.3 4.2 %collective-permute-done = f32[2,32,8,1]{3,2,1,0:T(8,128)S(1)} collective-permute-done((f32[2,32,8,1]{3,2,1,0:T(8,128)S(1)}, f32[2,32,8,1]{3,2,1,0:T(8,128)S(1)}, u32[]{:S(2)}, u32[]{:S(2)}) %collective-permute-start) | collective-permute-done | bytes 2080 | tf_op jit(solution)/shard_map/ppermute | solution.py:25
  12.6 4.1 %collective-permute-done.1 = f32[2,32,8,1]{3,2,1,0:T(8,128)S(1)} collective-permute-done((f32[2,32,8,1]{3,2,1,0:T(8,128)S(1)}, f32[2,32,8,1]{3,2,1,0:T(8,128)S(1)}, u32[]{:S(2)}, u32[]{:S(2)}) %collective-permute-start.1) | collective-permute-done | bytes 2080 | tf_op jit(solution)/shard_map/ppermute | solution.py:27
  17.2 3.5 collective-permute-start.2
  22.6 4.3 %collective-permute-done.3 = f32[2,32,1,130]{3,2,1,0:T(1,128)S(1)} collective-permute-done((f32[2,32,1,130]{3,2,1,0:T(1,128)S(1)}, f32[2,32,1,130]{3,2,1,0:T(1,128)S(1)}, u32[]{:S(2)}, u32[]{:S(2)}) %collective-permute-start.3) | collective-permute-done | bytes 33312 | tf_op jit(solution)/shard_map/ppermute | solution.py:27
  30.0 3.5 collective-permute-done.5
  38.1 3.7 %collective-permute-done.6 = f32[2,32,8,1]{3,2,1,0:T(8,128)S(1)} collective-permute-done((f32[2,32,8,1]{3,2,1,0:T(8,128)S(1)}, f32[2,32,8,1]{3,2,1,0:T(8,128)S(1)}, u32[]{:S(2)}, u32[]{:S(2)}) %collective-permute-start.6) | collective-permute-done | bytes 2080 | tf_op jit(solution)/shard_map/ppermute | solution.py:25
  41.8 4.7 %collective-permute-done.7 = f32[2,32,8,1]{3,2,1,0:T(8,128)S(1)} collective-permute-done((f32[2,32,8,1]{3,2,1,0:T(8,128)S(1)}, f32[2,32,8,1]{3,2,1,0:T(8,128)S(1)}, u32[]{:S(2)}, u32[]{:S(2)}) %collective-permute-start.7) | collective-permute-done | bytes 2080 | tf_op jit(solution)/shard_map/ppermute | solution.py:27
  46.9 3.5 collective-permute-start.8
  51.7 9.8 %reshape_broadcast_in_dim.3 = f32[16,2,4,2,64,2]{5,4,3,2,1,0:T(8,128)} reshape(f32[32,8,128]{2,1,0:T(8,128)S(1)} %get-tuple-element.41) | data formatting | bytes 262144 | tf_op jit(solution)/shard_map/reshape;broadcast_in_dim | solution.py:56
  61.5 4.0 %reduce_sum.71 = f32[16,4,64]{2,1,0:T(4,128)S(1)} reduce(f32[16,2,4,2,64,2]{5,4,3,2,1,0:T(8,128)} %reshape_broadcast_in_dim.3, f32[]{:T(128)} %constant.38.clone.1), dimensions={1,3,5}, to_apply=%region_1.0 | reduce | flops 28672 | bytes 147460 | tf_op jit(solution)/shard_map/reduce_sum | solution.py:58
  66.1 2.8 collective-permute-start.10
  73.7 18.1 %reshape.120 = f32[2,16,2,4,2,64,2]{6,5,4,3,2,1,0:T(8,128)} reshape(f32[2,32,8,128]{3,2,1,0:T(8,128)S(1)} %fusion.40) | data formatting | bytes 524288 | tf_op jit(solution)/shard_map/reshape | solution.py:56
  91.8 7.0 %reduce_sum.70 = f32[2,16,4,64]{3,2,1,0:T(4,128)S(1)} reduce(f32[2,16,2,4,2,64,2]{6,5,4,3,2,1,0:T(8,128)} %reshape.120, f32[]{:T(128)} %constant.38.clone.1), dimensions={2,4,6}, to_apply=%region_0.0 | reduce | flops 57344 | bytes 294916 | tf_op jit(solution)/shard_map/reduce_sum | solution.py:58
  102.5 4.3 %collective-permute-done.13 = f32[2,16,4,1]{3,1,2,0:T(8,128)S(1)} collective-permute-done((f32[2,16,4,1]{3,1,2,0:T(8,128)S(1)}, f32[2,16,4,1]{3,1,2,0:T(8,128)S(1)}, u32[]{:S(2)}, u32[]{:S(2)}) %collective-permute-start.13) | collective-permute-done | bytes 544 | tf_op jit(solution)/shard_map/ppermute | solution.py:27
  106.9 4.3 %collective-permute-start.14 = (f32[2,16,1,66]{3,1,2,0:T(8,128)S(1)}, f32[2,16,1,66]{3,1,2,0:T(8,128)S(1)}, u32[]{:S(2)}, u32[]{:S(2)}) collective-permute-start(f32[2,16,1,66]{3,1,2,0:T(8,128)S(1)} %get-tuple-element.39), channel_id=1, source_target_pairs={{0,4},{4,8},{8,12},{1,5},{5,9},{9,13},{2,6},{6,10},{10,14},{3,7},{... | collective-permute-start | bytes 25352 | tf_op jit(solution)/shard_map/ppermute | solution.py:25
  112.6 4.2 %collective-permute-done.15 = f32[2,16,1,66]{3,1,2,0:T(8,128)S(1)} collective-permute-done((f32[2,16,1,66]{3,1,2,0:T(8,128)S(1)}, f32[2,16,1,66]{3,1,2,0:T(8,128)S(1)}, u32[]{:S(2)}, u32[]{:S(2)}) %collective-permute-start.15) | collective-permute-done | bytes 8480 | tf_op jit(solution)/shard_map/ppermute | solution.py:27
  119.6 4.0 %collective-permute-done.17 = f32[2,1,6,66]{3,1,2,0:T(1,128)S(1)} collective-permute-done((f32[2,1,6,66]{3,1,2,0:T(1,128)S(1)}, f32[2,1,6,66]{3,1,2,0:T(1,128)S(1)}, u32[]{:S(2)}, u32[]{:S(2)}) %collective-permute-start.17) | collective-permute-done | bytes 3200 | tf_op jit(solution)/shard_map/ppermute | solution.py:27
  128.3 3.4 collective-permute-done.19
  131.8 3.5 collective-permute-start.20
  136.7 4.6 %all-gather = f32[8,2,64]{0,1,2:T(2,128)S(1)} all-gather(f32[8,2,32]{0,1,2:T(2,128)S(1)} %copy.381), channel_id=2, replica_groups=mesh['gx'=2,'gy'=4,'gz'=4] {'gx'}, dimensions={2}, use_global_device_ids=true | all-gather | bytes 6144 | tf_op jit(solution)/shard_map/all_gather | solution.py:96
  144.7 3.6 collective-permute-done.23
  151.2 4.9 %all_gather.6 = f32[2,8,2,64]{1,2,0,3:T(2,128)S(1)} all-gather(f32[2,8,2,32]{1,2,0,3:T(2,128)S(1)} %copy.379), channel_id=1, replica_groups=mesh['gx'=2,'gy'=4,'gz'=4] {'gx'}, dimensions={3}, use_global_device_ids=true | all-gather | bytes 12288 | tf_op jit(solution)/shard_map/all_gather | solution.py:95
  156.2 4.6 %collective-permute-start.24 = (f32[2,8,1,64]{3,1,2,0:T(8,128)S(1)}, f32[2,8,1,64]{3,1,2,0:T(8,128)S(1)}, u32[]{:S(2)}, u32[]{:S(2)}) collective-permute-start(f32[2,8,1,64]{3,1,2,0:T(8,128)S(1)} %get-tuple-element.76), channel_id=1, source_target_pairs={{0,4},{4,8},{8,12},{1,5},{5,9},{9,13},{2,6},{6,10},{10,14},{3,7},{... | collective-permute-start | bytes 12296 | tf_op jit(solution)/shard_map/ppermute | solution.py:25
  162.1 4.3 %collective-permute-done.25 = f32[2,8,1,64]{3,1,2,0:T(8,128)S(1)} collective-permute-done((f32[2,8,1,64]{3,1,2,0:T(8,128)S(1)}, f32[2,8,1,64]{3,1,2,0:T(8,128)S(1)}, u32[]{:S(2)}, u32[]{:S(2)}) %collective-permute-start.25) | collective-permute-done | bytes 4128 | tf_op jit(solution)/shard_map/ppermute | solution.py:27
  169.8 3.5 collective-permute-done.27
  177.1 3.9 %collective-permute-done.29 = f32[2,8,1,64]{3,1,2,0:T(8,128)S(1)} collective-permute-done((f32[2,8,1,64]{3,1,2,0:T(8,128)S(1)}, f32[2,8,1,64]{3,1,2,0:T(8,128)S(1)}, u32[]{:S(2)}, u32[]{:S(2)}) %collective-permute-start.29) | collective-permute-done | bytes 4128 | tf_op jit(solution)/shard_map/ppermute | solution.py:27
  181.1 2.8 collective-permute-start.30
  191.8 4.2 %collective-permute-done.33 = f32[2,4,1,32]{3,1,0,2:T(4,128)S(1)} collective-permute-done((f32[2,4,1,32]{3,1,0,2:T(4,128)S(1)}, f32[2,4,1,32]{3,1,0,2:T(4,128)S(1)}, u32[]{:S(2)}, u32[]{:S(2)}) %collective-permute-start.33) | collective-permute-done | bytes 1056 | tf_op jit(solution)/shard_map/ppermute | solution.py:27
  196.0 2.8 collective-permute-start.34
  206.3 4.2 %collective-permute-done.37 = f32[2,4,1,32]{3,1,0,2:T(4,128)S(1)} collective-permute-done((f32[2,4,1,32]{3,1,0,2:T(4,128)S(1)}, f32[2,4,1,32]{3,1,0,2:T(4,128)S(1)}, u32[]{:S(2)}, u32[]{:S(2)}) %collective-permute-start.37) | collective-permute-done | bytes 1056 | tf_op jit(solution)/shard_map/ppermute | solution.py:27
  220.9 4.2 %collective-permute-done.41 = f32[2,4,1,32]{3,1,0,2:T(4,128)S(1)} collective-permute-done((f32[2,4,1,32]{3,1,0,2:T(4,128)S(1)}, f32[2,4,1,32]{3,1,0,2:T(4,128)S(1)}, u32[]{:S(2)}, u32[]{:S(2)}) %collective-permute-start.41) | collective-permute-done | bytes 1056 | tf_op jit(solution)/shard_map/ppermute | solution.py:27
  225.1 2.8 collective-permute-start.42
  235.6 4.2 %collective-permute-done.45 = f32[2,8,1,64]{3,1,2,0:T(8,128)S(1)} collective-permute-done((f32[2,8,1,64]{3,1,2,0:T(8,128)S(1)}, f32[2,8,1,64]{3,1,2,0:T(8,128)S(1)}, u32[]{:S(2)}, u32[]{:S(2)}) %collective-permute-start.45) | collective-permute-done | bytes 4128 | tf_op jit(solution)/shard_map/ppermute | solution.py:27
  250.2 4.2 %collective-permute-done.49 = f32[2,8,1,64]{3,1,2,0:T(8,128)S(1)} collective-permute-done((f32[2,8,1,64]{3,1,2,0:T(8,128)S(1)}, f32[2,8,1,64]{3,1,2,0:T(8,128)S(1)}, u32[]{:S(2)}, u32[]{:S(2)}) %collective-permute-start.49) | collective-permute-done | bytes 4128 | tf_op jit(solution)/shard_map/ppermute | solution.py:27
  254.4 2.8 collective-permute-start.50
  265.9 4.3 %collective-permute-done.53 = f32[2,16,4,1]{3,1,2,0:T(8,128)S(1)} collective-permute-done((f32[2,16,4,1]{3,1,2,0:T(8,128)S(1)}, f32[2,16,4,1]{3,1,2,0:T(8,128)S(1)}, u32[]{:S(2)}, u32[]{:S(2)}) %collective-permute-start.53) | collective-permute-done | bytes 544 | tf_op jit(solution)/shard_map/ppermute | solution.py:27
  273.6 4.2 %collective-permute-done.55 = f32[2,16,1,66]{3,1,2,0:T(8,128)S(1)} collective-permute-done((f32[2,16,1,66]{3,1,2,0:T(8,128)S(1)}, f32[2,16,1,66]{3,1,2,0:T(8,128)S(1)}, u32[]{:S(2)}, u32[]{:S(2)}) %collective-permute-start.55) | collective-permute-done | bytes 8480 | tf_op jit(solution)/shard_map/ppermute | solution.py:27
  280.6 4.2 %collective-permute-done.57 = f32[2,1,6,66]{3,1,2,0:T(1,128)S(1)} collective-permute-done((f32[2,1,6,66]{3,1,2,0:T(1,128)S(1)}, f32[2,1,6,66]{3,1,2,0:T(1,128)S(1)}, u32[]{:S(2)}, u32[]{:S(2)}) %collective-permute-start.57) | collective-permute-done | bytes 3200 | tf_op jit(solution)/shard_map/ppermute | solution.py:27
  288.7 4.3 %collective-permute-done.59 = f32[2,16,4,1]{3,1,2,0:T(8,128)S(1)} collective-permute-done((f32[2,16,4,1]{3,1,2,0:T(8,128)S(1)}, f32[2,16,4,1]{3,1,2,0:T(8,128)S(1)}, u32[]{:S(2)}, u32[]{:S(2)}) %collective-permute-start.59) | collective-permute-done | bytes 544 | tf_op jit(solution)/shard_map/ppermute | solution.py:27
  296.4 4.2 %collective-permute-done.61 = f32[2,16,1,66]{3,1,2,0:T(8,128)S(1)} collective-permute-done((f32[2,16,1,66]{3,1,2,0:T(8,128)S(1)}, f32[2,16,1,66]{3,1,2,0:T(8,128)S(1)}, u32[]{:S(2)}, u32[]{:S(2)}) %collective-permute-start.61) | collective-permute-done | bytes 8480 | tf_op jit(solution)/shard_map/ppermute | solution.py:27
  303.5 4.2 %collective-permute-done.63 = f32[2,1,6,66]{3,1,2,0:T(1,128)S(1)} collective-permute-done((f32[2,1,6,66]{3,1,2,0:T(1,128)S(1)}, f32[2,1,6,66]{3,1,2,0:T(1,128)S(1)}, u32[]{:S(2)}, u32[]{:S(2)}) %collective-permute-start.63) | collective-permute-done | bytes 3200 | tf_op jit(solution)/shard_map/ppermute | solution.py:27
  311.8 4.0 %collective-permute-done.64 = f32[2,32,8,1]{3,2,1,0:T(8,128)S(1)} collective-permute-done((f32[2,32,8,1]{3,2,1,0:T(8,128)S(1)}, f32[2,32,8,1]{3,2,1,0:T(8,128)S(1)}, u32[]{:S(2)}, u32[]{:S(2)}) %collective-permute-start.64) | collective-permute-done | bytes 2080 | tf_op jit(solution)/shard_map/ppermute | solution.py:25
  315.8 4.7 %collective-permute-done.65 = f32[2,32,8,1]{3,2,1,0:T(8,128)S(1)} collective-permute-done((f32[2,32,8,1]{3,2,1,0:T(8,128)S(1)}, f32[2,32,8,1]{3,2,1,0:T(8,128)S(1)}, u32[]{:S(2)}, u32[]{:S(2)}) %collective-permute-start.65) | collective-permute-done | bytes 2080 | tf_op jit(solution)/shard_map/ppermute | solution.py:27
  325.3 4.1 %collective-permute-done.67 = f32[2,32,1,130]{3,2,1,0:T(1,128)S(1)} collective-permute-done((f32[2,32,1,130]{3,2,1,0:T(1,128)S(1)}, f32[2,32,1,130]{3,2,1,0:T(1,128)S(1)}, u32[]{:S(2)}, u32[]{:S(2)}) %collective-permute-start.67) | collective-permute-done | bytes 33312 | tf_op jit(solution)/shard_map/ppermute | solution.py:27
  340.2 4.0 %collective-permute-done.70 = f32[2,32,8,1]{3,2,1,0:T(8,128)S(1)} collective-permute-done((f32[2,32,8,1]{3,2,1,0:T(8,128)S(1)}, f32[2,32,8,1]{3,2,1,0:T(8,128)S(1)}, u32[]{:S(2)}, u32[]{:S(2)}) %collective-permute-start.70) | collective-permute-done | bytes 2080 | tf_op jit(solution)/shard_map/ppermute | solution.py:25
  344.2 4.7 %collective-permute-done.71 = f32[2,32,8,1]{3,2,1,0:T(8,128)S(1)} collective-permute-done((f32[2,32,8,1]{3,2,1,0:T(8,128)S(1)}, f32[2,32,8,1]{3,2,1,0:T(8,128)S(1)}, u32[]{:S(2)}, u32[]{:S(2)}) %collective-permute-start.71) | collective-permute-done | bytes 2080 | tf_op jit(solution)/shard_map/ppermute | solution.py:27
  353.3 4.1 %collective-permute-done.73 = f32[2,32,1,130]{3,2,1,0:T(1,128)S(1)} collective-permute-done((f32[2,32,1,130]{3,2,1,0:T(1,128)S(1)}, f32[2,32,1,130]{3,2,1,0:T(1,128)S(1)}, u32[]{:S(2)}, u32[]{:S(2)}) %collective-permute-start.73) | collective-permute-done | bytes 33312 | tf_op jit(solution)/shard_map/ppermute | solution.py:27
  (269 shorter events, 149.1 us)
Async XLA Ops:
  2.1 10.5 %collective-permute-start = (f32[2,32,8,1]{3,2,1,0:T(8,128)S(1)}, f32[2,32,8,1]{3,2,1,0:T(8,128)S(1)}, u32[]{:S(2)}, u32[]{:S(2)}) collective-permute-start(f32[2,32,8,1]{3,2,1,0:T(8,128)S(1)} %get-tuple-element.31), channel_id=1, source_target_pairs={{0,16},{1,17},{2,18},{3,19},{4,20},{5,21},{6,22},{7,23},{8,24},{9,... | collective-permute-start | bytes 6152 | tf_op jit(solution)/shard_map/ppermute | solution.py:25
  7.0 9.7 %collective-permute-start.1 = (f32[2,32,8,1]{3,2,1,0:T(8,128)S(1)}, f32[2,32,8,1]{3,2,1,0:T(8,128)S(1)}, u32[]{:S(2)}, u32[]{:S(2)}) collective-permute-start(f32[2,32,8,1]{3,2,1,0:T(8,128)S(1)} %get-tuple-element.32), channel_id=1, source_target_pairs={{16,0},{17,1},{18,2},{19,3},{20,4},{21,5},{22,6},{23,7},{24,8},{25... | collective-permute-start | bytes 6152 | tf_op jit(solution)/shard_map/ppermute | solution.py:27
  17.2 5.4 %collective-permute-start.2 = (f32[2,32,1,130]{3,2,1,0:T(1,128)S(1)}, f32[2,32,1,130]{3,2,1,0:T(1,128)S(1)}, u32[]{:S(2)}, u32[]{:S(2)}) collective-permute-start(f32[2,32,1,130]{3,2,1,0:T(1,128)S(1)} %get-tuple-element.23), channel_id=1, source_target_pairs={{0,4},{4,8},{8,12},{1,5},{5,9},{9,13},{2,6},{6,10},{10,14},{3,7},{... | collective-permute-start | bytes 99848 | tf_op jit(solution)/shard_map/ppermute | solution.py:25
  20.7 6.2 %collective-permute-start.3 = (f32[2,32,1,130]{3,2,1,0:T(1,128)S(1)}, f32[2,32,1,130]{3,2,1,0:T(1,128)S(1)}, u32[]{:S(2)}, u32[]{:S(2)}) collective-permute-start(f32[2,32,1,130]{3,2,1,0:T(1,128)S(1)} %get-tuple-element.24), channel_id=1, source_target_pairs={{4,0},{8,4},{12,8},{5,1},{9,5},{13,9},{6,2},{10,6},{14,10},{7,3},{... | collective-permute-start | bytes 99848 | tf_op jit(solution)/shard_map/ppermute | solution.py:27
  28.7 4.8 %collective-permute-start.5 = (f32[2,1,10,130]{3,0,2,1:T(2,128)S(1)}, f32[2,1,10,130]{3,0,2,1:T(2,128)S(1)}, u32[]{:S(2)}, u32[]{:S(2)}) collective-permute-start(f32[2,1,10,130]{3,0,2,1:T(2,128)S(1)} %copy.368), channel_id=1, source_target_pairs={{1,0},{2,1},{3,2},{5,4},{6,5},{7,6},{9,8},{10,9},{11,10},{13,12},{... | collective-permute-start | bytes 31208 | tf_op jit(solution)/shard_map/ppermute | solution.py:27
  35.3 6.5 %collective-permute-start.6 = (f32[2,32,8,1]{3,2,1,0:T(8,128)S(1)}, f32[2,32,8,1]{3,2,1,0:T(8,128)S(1)}, u32[]{:S(2)}, u32[]{:S(2)}) collective-permute-start(f32[2,32,8,1]{3,2,1,0:T(8,128)S(1)} %get-tuple-element.29), channel_id=1, source_target_pairs={{0,16},{1,17},{2,18},{3,19},{4,20},{5,21},{6,22},{7,23},{8,24},{9,... | collective-permute-start | bytes 6152 | tf_op jit(solution)/shard_map/ppermute | solution.py:25
  36.8 9.7 %collective-permute-start.7 = (f32[2,32,8,1]{3,2,1,0:T(8,128)S(1)}, f32[2,32,8,1]{3,2,1,0:T(8,128)S(1)}, u32[]{:S(2)}, u32[]{:S(2)}) collective-permute-start(f32[2,32,8,1]{3,2,1,0:T(8,128)S(1)} %get-tuple-element.30), channel_id=1, source_target_pairs={{16,0},{17,1},{18,2},{19,3},{20,4},{21,5},{22,6},{23,7},{24,8},{25... | collective-permute-start | bytes 6152 | tf_op jit(solution)/shard_map/ppermute | solution.py:27
  46.9 18.6 %collective-permute-start.8 = (f32[2,32,1,130]{3,2,1,0:T(1,128)S(1)}, f32[2,32,1,130]{3,2,1,0:T(1,128)S(1)}, u32[]{:S(2)}, u32[]{:S(2)}) collective-permute-start(f32[2,32,1,130]{3,2,1,0:T(1,128)S(1)} %get-tuple-element.21), channel_id=1, source_target_pairs={{0,4},{4,8},{8,12},{1,5},{5,9},{9,13},{2,6},{6,10},{10,14},{3,7},{... | collective-permute-start | bytes 99848 | tf_op jit(solution)/shard_map/ppermute | solution.py:25
  50.4 15.1 %collective-permute-start.9 = (f32[2,32,1,130]{3,2,1,0:T(1,128)S(1)}, f32[2,32,1,130]{3,2,1,0:T(1,128)S(1)}, u32[]{:S(2)}, u32[]{:S(2)}) collective-permute-start(f32[2,32,1,130]{3,2,1,0:T(1,128)S(1)} %get-tuple-element.22), channel_id=1, source_target_pairs={{4,0},{8,4},{12,8},{5,1},{9,5},{13,9},{6,2},{10,6},{14,10},{7,3},{... | collective-permute-start | bytes 99848 | tf_op jit(solution)/shard_map/ppermute | solution.py:27
  66.1 4.2 %collective-permute-start.10 = (f32[2,1,10,130]{3,0,2,1:T(2,128)S(1)}, f32[2,1,10,130]{3,0,2,1:T(2,128)S(1)}, u32[]{:S(2)}, u32[]{:S(2)}) collective-permute-start(f32[2,1,10,130]{3,0,2,1:T(2,128)S(1)} %copy.370), channel_id=1, source_target_pairs={{0,1},{1,2},{2,3},{4,5},{5,6},{6,7},{8,9},{9,10},{10,11},{12,13},{... | collective-permute-start | bytes 31208 | tf_op jit(solution)/shard_map/ppermute | solution.py:25
  100.6 6.2 %collective-permute-start.13 = (f32[2,16,4,1]{3,1,2,0:T(8,128)S(1)}, f32[2,16,4,1]{3,1,2,0:T(8,128)S(1)}, u32[]{:S(2)}, u32[]{:S(2)}) collective-permute-start(f32[2,16,4,1]{3,1,2,0:T(8,128)S(1)} %get-tuple-element.60), channel_id=1, source_target_pairs={{16,0},{17,1},{18,2},{19,3},{20,4},{21,5},{22,6},{23,7},{24,8},{25... | collective-permute-start | bytes 1544 | tf_op jit(solution)/shard_map/ppermute | solution.py:27
  106.9 5.7 %collective-permute-start.14 = (f32[2,16,1,66]{3,1,2,0:T(8,128)S(1)}, f32[2,16,1,66]{3,1,2,0:T(8,128)S(1)}, u32[]{:S(2)}, u32[]{:S(2)}) collective-permute-start(f32[2,16,1,66]{3,1,2,0:T(8,128)S(1)} %get-tuple-element.39), channel_id=1, source_target_pairs={{0,4},{4,8},{8,12},{1,5},{5,9},{9,13},{2,6},{6,10},{10,14},{3,7},{... | collective-permute-start | bytes 25352 | tf_op jit(solution)/shard_map/ppermute | solution.py:25
  111.2 5.6 %collective-permute-start.15 = (f32[2,16,1,66]{3,1,2,0:T(8,128)S(1)}, f32[2,16,1,66]{3,1,2,0:T(8,128)S(1)}, u32[]{:S(2)}, u32[]{:S(2)}) collective-permute-start(f32[2,16,1,66]{3,1,2,0:T(8,128)S(1)} %get-tuple-element.40), channel_id=1, source_target_pairs={{4,0},{8,4},{12,8},{5,1},{9,5},{13,9},{6,2},{10,6},{14,10},{7,3},{... | collective-permute-start | bytes 25352 | tf_op jit(solution)/shard_map/ppermute | solution.py:27
  118.3 5.3 %collective-permute-start.17 = (f32[2,1,6,66]{3,1,2,0:T(1,128)S(1)}, f32[2,1,6,66]{3,1,2,0:T(1,128)S(1)}, u32[]{:S(2)}, u32[]{:S(2)}) collective-permute-start(f32[2,1,6,66]{3,1,2,0:T(1,128)S(1)} %get-tuple-element.50), channel_id=1, source_target_pairs={{1,0},{2,1},{3,2},{5,4},{6,5},{7,6},{9,8},{10,9},{11,10},{13,12},{... | collective-permute-start | bytes 9512 | tf_op jit(solution)/shard_map/ppermute | solution.py:27
  124.0 4.3 %collective-permute-start.18 = (f32[2,16,4,1]{3,1,2,0:T(8,128)S(1)}, f32[2,16,4,1]{3,1,2,0:T(8,128)S(1)}, u32[]{:S(2)}, u32[]{:S(2)}) collective-permute-start(f32[2,16,4,1]{3,1,2,0:T(8,128)S(1)} %get-tuple-element.57), channel_id=1, source_target_pairs={{0,16},{1,17},{2,18},{3,19},{4,20},{5,21},{6,22},{7,23},{8,24},{9,... | collective-permute-start | bytes 1544 | tf_op jit(solution)/shard_map/ppermute | solution.py:25
  125.6 6.2 %collective-permute-start.19 = (f32[2,16,4,1]{3,1,2,0:T(8,128)S(1)}, f32[2,16,4,1]{3,1,2,0:T(8,128)S(1)}, u32[]{:S(2)}, u32[]{:S(2)}) collective-permute-start(f32[2,16,4,1]{3,1,2,0:T(8,128)S(1)} %get-tuple-element.58), channel_id=1, source_target_pairs={{16,0},{17,1},{18,2},{19,3},{20,4},{21,5},{22,6},{23,7},{24,8},{25... | collective-permute-start | bytes 1544 | tf_op jit(solution)/shard_map/ppermute | solution.py:27
  131.8 9.5 %collective-permute-start.20 = (f32[2,16,1,66]{3,1,2,0:T(8,128)S(1)}, f32[2,16,1,66]{3,1,2,0:T(8,128)S(1)}, u32[]{:S(2)}, u32[]{:S(2)}) collective-permute-start(f32[2,16,1,66]{3,1,2,0:T(8,128)S(1)} %get-tuple-element.37), channel_id=1, source_target_pairs={{0,4},{4,8},{8,12},{1,5},{5,9},{9,13},{2,6},{6,10},{10,14},{3,7},{... | collective-permute-start | bytes 25352 | tf_op jit(solution)/shard_map/ppermute | solution.py:25
  135.3 6.0 %collective-permute-start.21 = (f32[2,16,1,66]{3,1,2,0:T(8,128)S(1)}, f32[2,16,1,66]{3,1,2,0:T(8,128)S(1)}, u32[]{:S(2)}, u32[]{:S(2)}) collective-permute-start(f32[2,16,1,66]{3,1,2,0:T(8,128)S(1)} %get-tuple-element.38), channel_id=1, source_target_pairs={{4,0},{8,4},{12,8},{5,1},{9,5},{13,9},{6,2},{10,6},{14,10},{7,3},{... | collective-permute-start | bytes 25352 | tf_op jit(solution)/shard_map/ppermute | solution.py:27
  143.2 5.1 %collective-permute-start.23 = (f32[2,1,6,66]{3,1,2,0:T(1,128)S(1)}, f32[2,1,6,66]{3,1,2,0:T(1,128)S(1)}, u32[]{:S(2)}, u32[]{:S(2)}) collective-permute-start(f32[2,1,6,66]{3,1,2,0:T(1,128)S(1)} %get-tuple-element.48), channel_id=1, source_target_pairs={{1,0},{2,1},{3,2},{5,4},{6,5},{7,6},{9,8},{10,9},{11,10},{13,12},{... | collective-permute-start | bytes 9512 | tf_op jit(solution)/shard_map/ppermute | solution.py:27
  156.2 5.9 %collective-permute-start.24 = (f32[2,8,1,64]{3,1,2,0:T(8,128)S(1)}, f32[2,8,1,64]{3,1,2,0:T(8,128)S(1)}, u32[]{:S(2)}, u32[]{:S(2)}) collective-permute-start(f32[2,8,1,64]{3,1,2,0:T(8,128)S(1)} %get-tuple-element.76), channel_id=1, source_target_pairs={{0,4},{4,8},{8,12},{1,5},{5,9},{9,13},{2,6},{6,10},{10,14},{3,7},{... | collective-permute-start | bytes 12296 | tf_op jit(solution)/shard_map/ppermute | solution.py:25
  160.7 5.6 %collective-permute-start.25 = (f32[2,8,1,64]{3,1,2,0:T(8,128)S(1)}, f32[2,8,1,64]{3,1,2,0:T(8,128)S(1)}, u32[]{:S(2)}, u32[]{:S(2)}) collective-permute-start(f32[2,8,1,64]{3,1,2,0:T(8,128)S(1)} %get-tuple-element.77), channel_id=1, source_target_pairs={{4,0},{8,4},{12,8},{5,1},{9,5},{13,9},{6,2},{10,6},{14,10},{7,3},{... | collective-permute-start | bytes 12296 | tf_op jit(solution)/shard_map/ppermute | solution.py:27
  168.4 4.8 %collective-permute-start.27 = (f32[2,1,4,64]{3,1,2,0:T(1,128)S(1)}, f32[2,1,4,64]{3,1,2,0:T(1,128)S(1)}, u32[]{:S(2)}, u32[]{:S(2)}) collective-permute-start(f32[2,1,4,64]{3,1,2,0:T(1,128)S(1)} %get-tuple-element.68), channel_id=1, source_target_pairs={{1,0},{2,1},{3,2},{5,4},{6,5},{7,6},{9,8},{10,9},{11,10},{13,12},{... | collective-permute-start | bytes 6152 | tf_op jit(solution)/shard_map/ppermute | solution.py:27
  175.5 5.5 %collective-permute-start.29 = (f32[2,8,1,64]{3,1,2,0:T(8,128)S(1)}, f32[2,8,1,64]{3,1,2,0:T(8,128)S(1)}, u32[]{:S(2)}, u32[]{:S(2)}) collective-permute-start(f32[2,8,1,64]{3,1,2,0:T(8,128)S(1)} %get-tuple-element.75), channel_id=1, source_target_pairs={{4,0},{8,4},{12,8},{5,1},{9,5},{13,9},{6,2},{10,6},{14,10},{7,3},{... | collective-permute-start | bytes 12296 | tf_op jit(solution)/shard_map/ppermute | solution.py:27
  181.1 4.2 %collective-permute-start.30 = (f32[2,1,4,64]{3,1,2,0:T(1,128)S(1)}, f32[2,1,4,64]{3,1,2,0:T(1,128)S(1)}, u32[]{:S(2)}, u32[]{:S(2)}) collective-permute-start(f32[2,1,4,64]{3,1,2,0:T(1,128)S(1)} %get-tuple-element.65), channel_id=1, source_target_pairs={{0,1},{1,2},{2,3},{4,5},{5,6},{6,7},{8,9},{9,10},{10,11},{12,13},{... | collective-permute-start | bytes 6152 | tf_op jit(solution)/shard_map/ppermute | solution.py:25
  190.5 5.5 %collective-permute-start.33 = (f32[2,4,1,32]{3,1,0,2:T(4,128)S(1)}, f32[2,4,1,32]{3,1,0,2:T(4,128)S(1)}, u32[]{:S(2)}, u32[]{:S(2)}) collective-permute-start(f32[2,4,1,32]{3,1,0,2:T(4,128)S(1)} %fusion.173), channel_id=1, source_target_pairs={{4,0},{8,4},{12,8},{5,1},{9,5},{13,9},{6,2},{10,6},{14,10},{7,3},{... | collective-permute-start | bytes 3080 | tf_op jit(solution)/shard_map/ppermute | solution.py:27
  196.0 4.1 %collective-permute-start.34 = (f32[2,1,3,32]{3,1,0,2:T(1,128)S(1)}, f32[2,1,3,32]{3,1,0,2:T(1,128)S(1)}, u32[]{:S(2)}, u32[]{:S(2)}) collective-permute-start(f32[2,1,3,32]{3,1,0,2:T(1,128)S(1)} %get-tuple-element.82), channel_id=1, source_target_pairs={{0,1},{1,2},{2,3},{4,5},{5,6},{6,7},{8,9},{9,10},{10,11},{12,13},{... | collective-permute-start | bytes 2312 | tf_op jit(solution)/shard_map/ppermute | solution.py:25
  205.0 5.5 %collective-permute-start.37 = (f32[2,4,1,32]{3,1,0,2:T(4,128)S(1)}, f32[2,4,1,32]{3,1,0,2:T(4,128)S(1)}, u32[]{:S(2)}, u32[]{:S(2)}) collective-permute-start(f32[2,4,1,32]{3,1,0,2:T(4,128)S(1)} %multiply_add_fusion.1), channel_id=1, source_target_pairs={{4,0},{8,4},{12,8},{5,1},{9,5},{13,9},{6,2},{10,6},{14,10},{7,3},{... | collective-permute-start | bytes 3080 | tf_op jit(solution)/shard_map/ppermute | solution.py:27
  210.5 4.1 %collective-permute-start.38 = (f32[2,1,3,32]{3,1,0,2:T(1,128)S(1)}, f32[2,1,3,32]{3,1,0,2:T(1,128)S(1)}, u32[]{:S(2)}, u32[]{:S(2)}) collective-permute-start(f32[2,1,3,32]{3,1,0,2:T(1,128)S(1)} %get-tuple-element.80), channel_id=1, source_target_pairs={{0,1},{1,2},{2,3},{4,5},{5,6},{6,7},{8,9},{9,10},{10,11},{12,13},{... | collective-permute-start | bytes 2312 | tf_op jit(solution)/shard_map/ppermute | solution.py:25
  219.6 5.5 %collective-permute-start.41 = (f32[2,4,1,32]{3,1,0,2:T(4,128)S(1)}, f32[2,4,1,32]{3,1,0,2:T(4,128)S(1)}, u32[]{:S(2)}, u32[]{:S(2)}) collective-permute-start(f32[2,4,1,32]{3,1,0,2:T(4,128)S(1)} %multiply_add_fusion), channel_id=1, source_target_pairs={{4,0},{8,4},{12,8},{5,1},{9,5},{13,9},{6,2},{10,6},{14,10},{7,3},{... | collective-permute-start | bytes 3080 | tf_op jit(solution)/shard_map/ppermute | solution.py:27
  225.1 4.1 %collective-permute-start.42 = (f32[2,1,3,32]{3,1,0,2:T(1,128)S(1)}, f32[2,1,3,32]{3,1,0,2:T(1,128)S(1)}, u32[]{:S(2)}, u32[]{:S(2)}) collective-permute-start(f32[2,1,3,32]{3,1,0,2:T(1,128)S(1)} %get-tuple-element.78), channel_id=1, source_target_pairs={{0,1},{1,2},{2,3},{4,5},{5,6},{6,7},{8,9},{9,10},{10,11},{12,13},{... | collective-permute-start | bytes 2312 | tf_op jit(solution)/shard_map/ppermute | solution.py:25
  234.3 5.5 %collective-permute-start.45 = (f32[2,8,1,64]{3,1,2,0:T(8,128)S(1)}, f32[2,8,1,64]{3,1,2,0:T(8,128)S(1)}, u32[]{:S(2)}, u32[]{:S(2)}) collective-permute-start(f32[2,8,1,64]{3,1,2,0:T(8,128)S(1)} %get-tuple-element.73), channel_id=1, source_target_pairs={{4,0},{8,4},{12,8},{5,1},{9,5},{13,9},{6,2},{10,6},{14,10},{7,3},{... | collective-permute-start | bytes 12296 | tf_op jit(solution)/shard_map/ppermute | solution.py:27
  239.8 4.1 %collective-permute-start.46 = (f32[2,1,4,64]{3,1,2,0:T(1,128)S(1)}, f32[2,1,4,64]{3,1,2,0:T(1,128)S(1)}, u32[]{:S(2)}, u32[]{:S(2)}) collective-permute-start(f32[2,1,4,64]{3,1,2,0:T(1,128)S(1)} %get-tuple-element.63), channel_id=1, source_target_pairs={{0,1},{1,2},{2,3},{4,5},{5,6},{6,7},{8,9},{9,10},{10,11},{12,13},{... | collective-permute-start | bytes 6152 | tf_op jit(solution)/shard_map/ppermute | solution.py:25
  242.7 4.0 %collective-permute-start.47 = (f32[2,1,4,64]{3,1,2,0:T(1,128)S(1)}, f32[2,1,4,64]{3,1,2,0:T(1,128)S(1)}, u32[]{:S(2)}, u32[]{:S(2)}) collective-permute-start(f32[2,1,4,64]{3,1,2,0:T(1,128)S(1)} %get-tuple-element.64), channel_id=1, source_target_pairs={{1,0},{2,1},{3,2},{5,4},{6,5},{7,6},{9,8},{10,9},{11,10},{13,12},{... | collective-permute-start | bytes 6152 | tf_op jit(solution)/shard_map/ppermute | solution.py:27
  248.9 5.5 %collective-permute-start.49 = (f32[2,8,1,64]{3,1,2,0:T(8,128)S(1)}, f32[2,8,1,64]{3,1,2,0:T(8,128)S(1)}, u32[]{:S(2)}, u32[]{:S(2)}) collective-permute-start(f32[2,8,1,64]{3,1,2,0:T(8,128)S(1)} %get-tuple-element.71), channel_id=1, source_target_pairs={{4,0},{8,4},{12,8},{5,1},{9,5},{13,9},{6,2},{10,6},{14,10},{7,3},{... | collective-permute-start | bytes 12296 | tf_op jit(solution)/shard_map/ppermute | solution.py:27
  254.4 4.2 %collective-permute-start.50 = (f32[2,1,4,64]{3,1,2,0:T(1,128)S(1)}, f32[2,1,4,64]{3,1,2,0:T(1,128)S(1)}, u32[]{:S(2)}, u32[]{:S(2)}) collective-permute-start(f32[2,1,4,64]{3,1,2,0:T(1,128)S(1)} %get-tuple-element.61), channel_id=1, source_target_pairs={{0,1},{1,2},{2,3},{4,5},{5,6},{6,7},{8,9},{9,10},{10,11},{12,13},{... | collective-permute-start | bytes 6152 | tf_op jit(solution)/shard_map/ppermute | solution.py:25
  264.0 6.2 %collective-permute-start.53 = (f32[2,16,4,1]{3,1,2,0:T(8,128)S(1)}, f32[2,16,4,1]{3,1,2,0:T(8,128)S(1)}, u32[]{:S(2)}, u32[]{:S(2)}) collective-permute-start(f32[2,16,4,1]{3,1,2,0:T(8,128)S(1)} %get-tuple-element.54), channel_id=1, source_target_pairs={{16,0},{17,1},{18,2},{19,3},{20,4},{21,5},{22,6},{23,7},{24,8},{25... | collective-permute-start | bytes 1544 | tf_op jit(solution)/shard_map/ppermute | solution.py:27
  272.2 5.6 %collective-permute-start.55 = (f32[2,16,1,66]{3,1,2,0:T(8,128)S(1)}, f32[2,16,1,66]{3,1,2,0:T(8,128)S(1)}, u32[]{:S(2)}, u32[]{:S(2)}) collective-permute-start(f32[2,16,1,66]{3,1,2,0:T(8,128)S(1)} %get-tuple-element.36), channel_id=1, source_target_pairs={{4,0},{8,4},{12,8},{5,1},{9,5},{13,9},{6,2},{10,6},{14,10},{7,3},{... | collective-permute-start | bytes 25352 | tf_op jit(solution)/shard_map/ppermute | solution.py:27
  279.3 5.5 %collective-permute-start.57 = (f32[2,1,6,66]{3,1,2,0:T(1,128)S(1)}, f32[2,1,6,66]{3,1,2,0:T(1,128)S(1)}, u32[]{:S(2)}, u32[]{:S(2)}) collective-permute-start(f32[2,1,6,66]{3,1,2,0:T(1,128)S(1)} %get-tuple-element.46), channel_id=1, source_target_pairs={{1,0},{2,1},{3,2},{5,4},{6,5},{7,6},{9,8},{10,9},{11,10},{13,12},{... | collective-permute-start | bytes 9512 | tf_op jit(solution)/shard_map/ppermute | solution.py:27
  286.8 6.2 %collective-permute-start.59 = (f32[2,16,4,1]{3,1,2,0:T(8,128)S(1)}, f32[2,16,4,1]{3,1,2,0:T(8,128)S(1)}, u32[]{:S(2)}, u32[]{:S(2)}) collective-permute-start(f32[2,16,4,1]{3,1,2,0:T(8,128)S(1)} %get-tuple-element.52), channel_id=1, source_target_pairs={{16,0},{17,1},{18,2},{19,3},{20,4},{21,5},{22,6},{23,7},{24,8},{25... | collective-permute-start | bytes 1544 | tf_op jit(solution)/shard_map/ppermute | solution.py:27
  295.0 5.6 %collective-permute-start.61 = (f32[2,16,1,66]{3,1,2,0:T(8,128)S(1)}, f32[2,16,1,66]{3,1,2,0:T(8,128)S(1)}, u32[]{:S(2)}, u32[]{:S(2)}) collective-permute-start(f32[2,16,1,66]{3,1,2,0:T(8,128)S(1)} %get-tuple-element.34), channel_id=1, source_target_pairs={{4,0},{8,4},{12,8},{5,1},{9,5},{13,9},{6,2},{10,6},{14,10},{7,3},{... | collective-permute-start | bytes 25352 | tf_op jit(solution)/shard_map/ppermute | solution.py:27
  302.1 5.5 %collective-permute-start.63 = (f32[2,1,6,66]{3,1,2,0:T(1,128)S(1)}, f32[2,1,6,66]{3,1,2,0:T(1,128)S(1)}, u32[]{:S(2)}, u32[]{:S(2)}) collective-permute-start(f32[2,1,6,66]{3,1,2,0:T(1,128)S(1)} %get-tuple-element.44), channel_id=1, source_target_pairs={{1,0},{2,1},{3,2},{5,4},{6,5},{7,6},{9,8},{10,9},{11,10},{13,12},{... | collective-permute-start | bytes 9512 | tf_op jit(solution)/shard_map/ppermute | solution.py:27
  308.9 6.8 %collective-permute-start.64 = (f32[2,32,8,1]{3,2,1,0:T(8,128)S(1)}, f32[2,32,8,1]{3,2,1,0:T(8,128)S(1)}, u32[]{:S(2)}, u32[]{:S(2)}) collective-permute-start(f32[2,32,8,1]{3,2,1,0:T(8,128)S(1)} %get-tuple-element.27), channel_id=1, source_target_pairs={{0,16},{1,17},{2,18},{3,19},{4,20},{5,21},{6,22},{7,23},{8,24},{9,... | collective-permute-start | bytes 6152 | tf_op jit(solution)/shard_map/ppermute | solution.py:25
  310.5 9.9 %collective-permute-start.65 = (f32[2,32,8,1]{3,2,1,0:T(8,128)S(1)}, f32[2,32,8,1]{3,2,1,0:T(8,128)S(1)}, u32[]{:S(2)}, u32[]{:S(2)}) collective-permute-start(f32[2,32,8,1]{3,2,1,0:T(8,128)S(1)} %get-tuple-element.28), channel_id=1, source_target_pairs={{16,0},{17,1},{18,2},{19,3},{20,4},{21,5},{22,6},{23,7},{24,8},{25... | collective-permute-start | bytes 6152 | tf_op jit(solution)/shard_map/ppermute | solution.py:27
  321.0 4.4 %collective-permute-start.66 = (f32[2,32,1,130]{3,2,1,0:T(1,128)S(1)}, f32[2,32,1,130]{3,2,1,0:T(1,128)S(1)}, u32[]{:S(2)}, u32[]{:S(2)}) collective-permute-start(f32[2,32,1,130]{3,2,1,0:T(1,128)S(1)} %get-tuple-element.19), channel_id=1, source_target_pairs={{0,4},{4,8},{8,12},{1,5},{5,9},{9,13},{2,6},{6,10},{10,14},{3,7},{... | collective-permute-start | bytes 99848 | tf_op jit(solution)/shard_map/ppermute | solution.py:25
  322.9 6.6 %collective-permute-start.67 = (f32[2,32,1,130]{3,2,1,0:T(1,128)S(1)}, f32[2,32,1,130]{3,2,1,0:T(1,128)S(1)}, u32[]{:S(2)}, u32[]{:S(2)}) collective-permute-start(f32[2,32,1,130]{3,2,1,0:T(1,128)S(1)} %get-tuple-element.20), channel_id=1, source_target_pairs={{4,0},{8,4},{12,8},{5,1},{9,5},{13,9},{6,2},{10,6},{14,10},{7,3},{... | collective-permute-start | bytes 99848 | tf_op jit(solution)/shard_map/ppermute | solution.py:27
  336.6 7.6 %collective-permute-start.70 = (f32[2,32,8,1]{3,2,1,0:T(8,128)S(1)}, f32[2,32,8,1]{3,2,1,0:T(8,128)S(1)}, u32[]{:S(2)}, u32[]{:S(2)}) collective-permute-start(f32[2,32,8,1]{3,2,1,0:T(8,128)S(1)} %get-tuple-element.25), channel_id=1, source_target_pairs={{0,16},{1,17},{2,18},{3,19},{4,20},{5,21},{6,22},{7,23},{8,24},{9,... | collective-permute-start | bytes 6152 | tf_op jit(solution)/shard_map/ppermute | solution.py:25
  338.7 10.2 %collective-permute-start.71 = (f32[2,32,8,1]{3,2,1,0:T(8,128)S(1)}, f32[2,32,8,1]{3,2,1,0:T(8,128)S(1)}, u32[]{:S(2)}, u32[]{:S(2)}) collective-permute-start(f32[2,32,8,1]{3,2,1,0:T(8,128)S(1)} %get-tuple-element.26), channel_id=1, source_target_pairs={{16,0},{17,1},{18,2},{19,3},{20,4},{21,5},{22,6},{23,7},{24,8},{25... | collective-permute-start | bytes 6152 | tf_op jit(solution)/shard_map/ppermute | solution.py:27
  350.9 6.5 %collective-permute-start.73 = (f32[2,32,1,130]{3,2,1,0:T(1,128)S(1)}, f32[2,32,1,130]{3,2,1,0:T(1,128)S(1)}, u32[]{:S(2)}, u32[]{:S(2)}) collective-permute-start(f32[2,32,1,130]{3,2,1,0:T(1,128)S(1)} %get-tuple-element.18), channel_id=1, source_target_pairs={{4,0},{8,4},{12,8},{5,1},{9,5},{13,9},{6,2},{10,6},{14,10},{7,3},{... | collective-permute-start | bytes 99848 | tf_op jit(solution)/shard_map/ppermute | solution.py:27
  (29 other events, 129.2 us)
where the time goes:
time: 369 us; the launch traced here: 365 us
  waiting for transfers between devices  154 us (42%)
  starting transfers between devices  137 us (37%)
  local copies, waits for them, and re-layouts  34.5 us (9%)
  other arithmetic  28.3 us (8%)
  blocking collectives  9.57 us (3%)
    ppermute x38, waiting for transfers between devices, with_halo(): lax.ppermute(head, axis, [((i + 1) % count, i) for i in range(ends)])  133 us
    ppermute x38, starting transfers between devices, with_halo(): lax.ppermute(tail, axis, [(i, (i + 1) % count) for i in range(ends)])  87.3 us
    ppermute x38, starting transfers between devices, with_halo(): lax.ppermute(head, axis, [((i + 1) % count, i) for i in range(ends)])  49.5 us
    ppermute x38, waiting for transfers between devices, with_halo(): lax.ppermute(tail, axis, [(i, (i + 1) % count) for i in range(ends)])  21.1 us
    reshape x2, local copies, waits for them, and re-layouts, restrict(): values.reshape(values.shape[0], values.shape[1] // 2, 2, values.shape[2]...  20.3 us
    reduce_sum x8, other arithmetic, restrict(): return values.reshape(values.shape[0], values.shape[1] // 2, 2, values.sh...  11.8 us
    another operation x1, local copies, waits for them, and re-layouts, restrict(): values.reshape(values.shape[0], values.shape[1] // 2, 2, values.shape[2]...  9.8 us
  transfers between devices with their start and end apart: 76, of which 49 were waited for; matrix products, arithmetic and copies ran while one was open for 4% of the time, Pallas kernels for 0%

commit v1 on v0

v1 whole, which is shorter than its diff:
```python
import math

import jax
import jax.numpy as jnp
from jax import lax
from jax.sharding import PartitionSpec as P

LEVELS = 8
middle_point = 0.646875
half_range = 0.503125
first_weight = 1.0 / (middle_point + half_range * math.cos(math.pi / 4))
second_weight = 1.0 / (middle_point - half_range * math.cos(math.pi / 4))
SIDES = (("gy", 2), ("gz", 1), ("gx", 3))


def with_halo(cells, width):
    for axis, dim in SIDES:
        count = lax.axis_size(axis)
        ends = count - 1
        head = lax.slice_in_dim(cells, 0, width, axis=dim)
        tail = lax.slice_in_dim(cells, cells.shape[dim] - width, cells.shape[dim], axis=dim)
        cells = jnp.concatenate(
            [
                lax.ppermute(tail, axis, [(i, i + 1) for i in range(ends)]),
                cells,
                lax.ppermute(head, axis, [(i + 1, i) for i in range(ends)]),
            ],
            axis=dim,
        )
    return cells


def crop(values, width):
    if width == 0:
        return values
    return values[:, width:-width, width:-width, width:-width]


def smooth_sum(padded):
    padded = 0.5 * (padded[:, :-2] + padded[:, 2:]) + padded[:, 1:-1]
    padded = 0.5 * (padded[:, :, :-2] + padded[:, :, 2:]) + padded[:, :, 1:-1]
    return 0.5 * (padded[..., :-2] + padded[..., 2:]) + padded[..., 1:-1]


def residue(padded, target, stiffness, spacing_sq):
    return target - stiffness * (16.0 * crop(padded, 1) - 2.0 * smooth_sum(padded)) * (1.0 / spacing_sq)


def step(padded, target, stiffness, inverse, weight, spacing_sq):
    return crop(padded, 1) + weight * inverse * residue(padded, target, stiffness, spacing_sq)


def invert(stiffness, spacing_sq):
    inside = stiffness > 0.0
    return jnp.where(inside, spacing_sq / (14.0 * jnp.where(inside, stiffness, 1.0)), 0.0)


def restrict(values):
    return values.reshape(
        values.shape[0], values.shape[1] // 2, 2, values.shape[2] // 2, 2, values.shape[3] // 2, 2
    ).mean(axis=(2, 4, 6))


def prolong(values):
    return jnp.repeat(jnp.repeat(jnp.repeat(values, 2, axis=1), 2, axis=2), 2, axis=3)


def pad(values, width=1):
    return jnp.pad(values, ((0, 0),) + ((width, width),) * 3)


def post(guess, target, stiffness, inverse, spacing_sq):
    guess = step(pad(guess), target, stiffness, inverse, first_weight, spacing_sq)
    return step(pad(guess), target, stiffness, inverse, second_weight, spacing_sq)


def pre(target, stiffness, inverse, spacing_sq):
    guess = first_weight * inverse * target
    return step(pad(guess), target, stiffness, inverse, second_weight, spacing_sq)


def coarse_cycle(rhs, stiffness):
    inverse = invert(stiffness, 16.0)
    guess = pre(rhs, stiffness, inverse, 16.0)
    rhs_base = restrict(residue(pad(guess), rhs, stiffness, 16.0))
    stiffness_base = restrict(stiffness)
    inverse_base = invert(stiffness_base, 64.0)
    guess_base = pre(rhs_base, stiffness_base, inverse_base, 64.0)
    guess_base = post(guess_base, rhs_base, stiffness_base, inverse_base, 64.0)
    return post(guess + prolong(guess_base), rhs, stiffness, inverse, 16.0)


def gather_all(block):
    counts = [lax.axis_size(axis) for axis in ("gz", "gy", "gx")]
    fields, z, y, x = block.shape
    whole = lax.all_gather(block, ("gz", "gy", "gx"), axis=0, tiled=False)
    whole = whole.reshape(*counts, fields, z, y, x).transpose(3, 0, 4, 1, 5, 2, 6)
    return whole.reshape(fields, counts[0] * z, counts[1] * y, counts[2] * x)


def body(load_cases, density_level):
    stiffness_own = (0.05 + 0.95 * (density_level.astype(jnp.float32) / (LEVELS - 1)) ** 3)[None]
    stiffness_mid_own = restrict(stiffness_own)
    stiffness_low = restrict(stiffness_mid_own)

    fine = with_halo(jnp.concatenate([load_cases, stiffness_own], axis=0), 3)
    target, stiffness = fine[:2], fine[2:]
    inverse = invert(stiffness, 1.0)
    guess_fine = step(
        first_weight * inverse * target, crop(target, 1), crop(stiffness, 1), crop(inverse, 1), second_weight, 1.0
    )
    rhs_mid_own = restrict(residue(crop(guess_fine, 1), load_cases, stiffness_own, 1.0))

    mid = with_halo(jnp.concatenate([rhs_mid_own, stiffness_mid_own], axis=0), 4)
    rhs_mid, stiffness_mid = mid[:2], mid[2:]
    inverse_mid = invert(stiffness_mid, 4.0)
    guess_mid = step(
        first_weight * inverse_mid * rhs_mid,
        crop(rhs_mid, 1), crop(stiffness_mid, 1), crop(inverse_mid, 1), second_weight, 4.0,
    )
    rhs_low = restrict(residue(crop(guess_mid, 2), rhs_mid_own, stiffness_mid_own, 4.0))

    own = rhs_low.shape
    low = gather_all(jnp.concatenate([rhs_low, stiffness_low], axis=0))
    guess_low = pad(coarse_cycle(low[:2], low[2:]), 2)
    starts = [0] + [lax.axis_index(axis) * size for axis, size in zip(("gz", "gy", "gx"), own[1:])]
    guess_low = lax.dynamic_slice(guess_low, starts, (own[0],) + tuple(size + 4 for size in own[1:]))

    guess_mid = guess_mid + crop(prolong(guess_low), 1)
    guess_mid = step(
        guess_mid, crop(rhs_mid, 2), crop(stiffness_mid, 2), crop(inverse_mid, 2), first_weight, 4.0
    )
    guess_mid = step(
        guess_mid, crop(rhs_mid, 3), crop(stiffness_mid, 3), crop(inverse_mid, 3), second_weight, 4.0
    )

    guess_fine = guess_fine + prolong(guess_mid)
    guess_fine = step(
        guess_fine, crop(target, 2), crop(stiffness, 2), crop(inverse, 2), first_weight, 1.0
    )
    return step(guess_fine, load_cases, stiffness_own, crop(inverse, 3), second_weight, 1.0)


def solution(mesh):
    in_specs = (P(None, "gz", "gy", "gx"), P("gz", "gy", "gx"))
    out_specs = P(None, "gz", "gy", "gx")
    return jax.shard_map(body, mesh=mesh, in_specs=in_specs, out_specs=out_specs, check_vma=False)
```

time: 369 us -> 254 us (0.69)
  waiting for transfers between devices: 154 us -> 28.4 us
  starting transfers between devices: 137 us -> 26 us
  blocking collectives: 9.57 us -> 68.5 us
  local copies, waits for them, and re-layouts: 34.5 us -> 82.1 us
  other arithmetic: 28.3 us -> 46.2 us
    ppermute x76 -> x12, waiting for transfers between devices: 154 us -> 28.4 us  [the longest x6 18.8 us: with_halo(): lax.ppermute(head, axis, [(i + 1, i) for i in range(ends)])]
    ppermute x76 -> x12, starting transfers between devices: 137 us -> 26 us  [the longest x6 18.1 us: with_halo(): lax.ppermute(tail, axis, [(i, i + 1) for i in range(ends)])]
    all_gather x2 -> x1, blocking collectives: 9.57 us -> 68.5 us  [gather_all(): whole = lax.all_gather(block, ('gz', 'gy', 'gx'), axis=0, tiled=False)]
    reshape x2 -> x3, local copies, waits for them, and re-layouts: 20.3 us -> 32.5 us  [restrict(): values.reshape(values.shape[0], values.shape[1] // 2, 2, values.shape[2]...]
    reduce_sum x8 -> x7, other arithmetic: 11.8 us -> 21.2 us  [restrict(): return values.reshape(values.shape[0], values.shape[1] // 2, 2, values.sh...]
    unnamed x2 -> x43, local copies, waits for them, and re-layouts: 0.01 us -> 6.18 us
    reshape x2, local copies, waits for them, and re-layouts: 0.47 us -> 5.58 us  [prolong(): jnp.repeat(jnp.repeat(jnp.repeat(values, 2, axis=1), 2, axis=2), 2, axis=3)]
    slice x0 -> x10, local copies, waits for them, and re-layouts: none -> 4.87 us  [the longest x4 2.82 us: crop(): return values[:, width:-width, width:-width, width:-width]]
  transfers between devices with their start and end apart: 76 -> 12, of which waited for: 49 -> 8; matrix products, arithmetic and copies ran while one was open for 4% -> 8% of each run, Pallas kernels for 0% -> 0%
where the time goes in v1:
time: 254 us; the launch traced here: 252 us
  local copies, waits for them, and re-layouts  82.1 us (32%)
  blocking collectives  68.5 us (27%)
  other arithmetic  46.2 us (18%)
  waiting for transfers between devices  28.4 us (11%)
  starting transfers between devices  26 us (10%)
    all_gather x1, blocking collectives, gather_all(): whole = lax.all_gather(block, ('gz', 'gy', 'gx'), axis=0, tiled=False)  68.5 us
    reshape x3, local copies, waits for them, and re-layouts, restrict(): values.reshape(values.shape[0], values.shape[1] // 2, 2, values.shape[2]...  32.5 us
    reduce_sum x7, other arithmetic, restrict(): return values.reshape(values.shape[0], values.shape[1] // 2, 2, values.sh...  21.2 us
    ppermute x6, waiting for transfers between devices, with_halo(): lax.ppermute(head, axis, [(i + 1, i) for i in range(ends)])  18.8 us
    ppermute x6, starting transfers between devices, with_halo(): lax.ppermute(tail, axis, [(i, i + 1) for i in range(ends)])  18.1 us
    another operation x1, local copies, waits for them, and re-layouts, restrict(): values.reshape(values.shape[0], values.shape[1] // 2, 2, values.shape[2]...  9.78 us
    ppermute x6, waiting for transfers between devices, with_halo(): lax.ppermute(tail, axis, [(i, i + 1) for i in range(ends)])  9.6 us
    ppermute x6, starting transfers between devices, with_halo(): lax.ppermute(head, axis, [(i + 1, i) for i in range(ends)])  7.92 us
  transfers between devices with their start and end apart: 12, of which 8 were waited for; matrix products, arithmetic and copies ran while one was open for 8% of the time, Pallas kernels for 0%

profile of v1, /device:TPU:0, one launch (start us, length us, event | category | flops | bytes accessed | tf_op | source)
XLA Modules:
  0.0 252.3 jit_solution(3213461905009716725)
XLA Ops:
  2.1 5.0 %collective-permute-start = (f32[3,32,3,128]{3,1,2,0:T(8,128)S(1)}, f32[3,32,3,128]{3,1,2,0:T(8,128)S(1)}, u32[]{:S(2)}, u32[]{:S(2)}) collective-permute-start(f32[3,32,3,128]{3,1,2,0:T(8,128)S(1)} %get-tuple-element.17), channel_id=1, source_target_pairs={{0,4},{4,8},{8,12},{1,5},{5,9},{9,13},{2,6},{6,10},{10,14},{3,7},{... | collective-permute-start | bytes 442376 | tf_op jit(solution)/shard_map/ppermute | solution.py:24
  7.0 1.3 collective-permute-start.1
  8.3 1.8 collective-permute-done
  10.1 4.1 %collective-permute-done.1 = f32[3,32,3,128]{3,1,2,0:T(8,128)S(1)} collective-permute-done((f32[3,32,3,128]{3,1,2,0:T(8,128)S(1)}, f32[3,32,3,128]{3,1,2,0:T(8,128)S(1)}, u32[]{:S(2)}, u32[]{:S(2)}) %collective-permute-start.1) | collective-permute-done | bytes 147488 | tf_op jit(solution)/shard_map/ppermute | solution.py:26
  14.3 1.3 collective-permute-start.2
  15.6 1.3 collective-permute-start.3
  17.0 9.8 %reshape_broadcast_in_dim.3 = f32[16,2,4,2,64,2]{5,4,3,2,1,0:T(8,128)} reshape(f32[32,8,128]{2,1,0:T(8,128)S(1)} %copy.87) | data formatting | bytes 262144 | tf_op jit(solution)/shard_map/reshape;broadcast_in_dim | solution.py:59
  26.7 4.0 %reduce_sum.62 = f32[16,4,64]{2,1,0:T(4,128)S(1)} reduce(f32[16,2,4,2,64,2]{5,4,3,2,1,0:T(8,128)} %reshape_broadcast_in_dim.3, f32[]{:T(128)} %constant.32.clone.1), dimensions={1,3,5}, to_apply=%region_1.0 | reduce | flops 28672 | bytes 147460 | tf_op jit(solution)/shard_map/reduce_sum | solution.py:61
  30.9 1.2 fusion.173
  32.1 1.6 copy.81
  33.7 3.4 %collective-permute-start.4 = (f32[3,38,14,3]{1,2,3,0:T(8,128)S(1)}, f32[3,38,14,3]{1,2,3,0:T(8,128)S(1)}, u32[]{:S(2)}, u32[]{:S(2)}) collective-permute-start(f32[3,38,14,3]{1,2,3,0:T(8,128)S(1)} %copy.81), channel_id=1, source_target_pairs={{0,16},{1,17},{2,18},{3,19},{4,20},{5,21},{6,22},{7,23},{8,24},{9,... | collective-permute-start | bytes 57464 | tf_op jit(solution)/shard_map/ppermute | solution.py:24
  37.6 1.3 collective-permute-start.5
  40.7 1.4 copy.83
  42.1 1.7 collective-permute-done.5
  43.8 1.3 copy.84
  45.2 2.3 pad_maximum_fusion
  48.5 1.2 fusion.7
  51.0 18.1 %reshape.135 = f32[2,16,2,4,2,64,2]{6,5,4,3,2,1,0:T(8,128)} reshape(f32[2,32,8,128]{3,2,1,0:T(8,128)S(1)} %copy.86) | data formatting | bytes 524288 | tf_op jit(solution)/shard_map/reshape | solution.py:59
  69.1 7.0 %reduce_sum.61 = f32[2,16,4,64]{3,2,1,0:T(4,128)S(1)} reduce(f32[2,16,2,4,2,64,2]{6,5,4,3,2,1,0:T(8,128)} %reshape.135, f32[]{:T(128)} %constant.32.clone.1), dimensions={2,4,6}, to_apply=%region_0.0 | reduce | flops 57344 | bytes 294916 | tf_op jit(solution)/shard_map/reduce_sum | solution.py:61
  76.2 3.5 %collective-permute-start.6 = (f32[3,16,4,64]{3,1,2,0:T(8,128)S(1)}, f32[3,16,4,64]{3,1,2,0:T(8,128)S(1)}, u32[]{:S(2)}, u32[]{:S(2)}) collective-permute-start(f32[3,16,4,64]{3,1,2,0:T(8,128)S(1)} %copy_dynamic-update-slice_fusion.1), channel_id=1, source_target_pairs={{0,4},{4,8},{8,12},{1,5},{5,9},{9,13},{2,6},{6,10},{10,14},{3,7},{... | collective-permute-start | bytes 147464 | tf_op jit(solution)/shard_map/ppermute | solution.py:24
  79.7 1.3 collective-permute-start.7
  81.0 1.4 collective-permute-done.6
  82.4 4.8 %collective-permute-done.7 = f32[3,16,4,64]{3,1,2,0:T(8,128)} collective-permute-done((f32[3,16,4,64]{3,1,2,0:T(8,128)S(1)}, f32[3,16,4,64]{3,1,2,0:T(8,128)}, u32[]{:S(2)}, u32[]{:S(2)}) %collective-permute-start.7) | collective-permute-done | bytes 49184 | tf_op jit(solution)/shard_map/ppermute | solution.py:26
  88.0 2.0 collective-permute-start.8
  90.1 1.5 collective-permute-start.9
  91.6 1.3 slice_bitcast_fusion.1
  92.8 3.5 %collective-permute-done.9 = f32[3,4,12,64]{3,1,2,0:T(4,128)S(1)} collective-permute-done((f32[3,4,12,64]{3,1,2,0:T(4,128)S(1)}, f32[3,4,12,64]{3,1,2,0:T(4,128)S(1)}, u32[]{:S(2)}, u32[]{:S(2)}) %collective-permute-start.9) | collective-permute-done | bytes 36896 | tf_op jit(solution)/shard_map/ppermute | solution.py:26
  97.5 2.9 %collective-permute-start.10 = (f32[3,24,12,4]{3,1,2,0:T(8,128)S(1)}, f32[3,24,12,4]{3,1,2,0:T(8,128)S(1)}, u32[]{:S(2)}, u32[]{:S(2)}) collective-permute-start(f32[3,24,12,4]{3,1,2,0:T(8,128)S(1)} %get-tuple-element.15), channel_id=1, source_target_pairs={{0,16},{1,17},{2,18},{3,19},{4,20},{5,21},{6,22},{7,23},{8,24},{9,... | collective-permute-start | bytes 41480 | tf_op jit(solution)/shard_map/ppermute | solution.py:24
  100.4 1.3 collective-permute-start.11
  102.4 6.4 %collective-permute-done.10 = f32[3,24,12,4]{3,1,2,0:T(8,128)S(1)} collective-permute-done((f32[3,24,12,4]{3,1,2,0:T(8,128)S(1)}, f32[3,24,12,4]{3,1,2,0:T(8,128)S(1)}, u32[]{:S(2)}, u32[]{:S(2)}) %collective-permute-start.10) | collective-permute-done | bytes 13856 | tf_op jit(solution)/shard_map/ppermute | solution.py:24
  108.8 4.7 %collective-permute-done.11 = f32[3,24,12,4]{3,1,2,0:T(8,128)S(1)} collective-permute-done((f32[3,24,12,4]{3,1,2,0:T(8,128)S(1)}, f32[3,24,12,4]{3,1,2,0:T(8,128)S(1)}, u32[]{:S(2)}, u32[]{:S(2)}) %collective-permute-start.11) | collective-permute-done | bytes 13856 | tf_op jit(solution)/shard_map/ppermute | solution.py:26
  113.5 1.3 pad_maximum_fusion.3
  116.9 3.5 %reshape.136 = f32[2,8,2,2,2,32,2]{6,5,2,1,4,3,0:T(8,128)} reshape(f32[2,16,4,64]{3,1,2,0:T(8,128)S(1)} %copy.95) | data formatting | bytes 65536 | tf_op jit(solution)/shard_map/reshape | solution.py:59
  120.4 1.8 reduce_sum.63
  122.2 68.5 %all-gather = f32[96,8,2,32]{3,1,2,0:T(8,128)S(1)} all-gather(f32[3,8,2,32]{3,1,2,0:T(8,128)S(1)} %pad_maximum_fusion.13), channel_id=2, replica_groups=mesh['gx'=2,'gy'=4,'gz'=4] {'gz','gy','gx'}, dimensions={0}, use_global_device_ids=true | all-gather | bytes 202752 | tf_op jit(solution)/shard_map/all_gather | solution.py:96
  190.8 1.4 slice_reduce_fusion
  200.9 10.9 %reshape.138 = f32[2,16,2,4,2,32,2]{6,5,4,3,2,1,0:T(8,128)} reshape(f32[2,32,8,64]{3,2,1,0:T(8,128)} %fusion.78) | data formatting | bytes 262144 | tf_op jit(solution)/shard_map/reshape | solution.py:59
  211.8 4.1 %reduce_sum.65 = f32[2,16,4,32]{3,2,1,0:T(4,128)S(1)} reduce(f32[2,16,2,4,2,32,2]{6,5,4,3,2,1,0:T(8,128)} %reshape.138, f32[]{:T(128)} %constant.32.clone.1), dimensions={2,4,6}, to_apply=%region_4.5 | reduce | flops 28672 | bytes 147460 | tf_op jit(solution)/shard_map/reduce_sum | solution.py:61
  215.9 2.4 copy.99
  218.2 2.8 %reduce_sum.68 = f32[16,4,32]{1,2,0:T(8,128)} reduce(f32[16,2,4,32,2]{2,4,3,1,0:T(2,128)} %bitcast.59, f32[]{:T(128)} %constant.32.clone.1), dimensions={1,4}, to_apply=%region_6.7 | reduce | flops 6144 | bytes 40964 | tf_op jit(solution)/shard_map/reduce_sum | solution.py:61
  221.0 1.7 copy.100
  225.4 1.7 copy.106
  228.9 1.9 copy.107
  235.5 1.6 copy.124
  239.6 1.5 copy.118
  241.1 1.6 broadcast_in_dim.60
  242.7 3.6 %copy.119 = f32[2,36,12,132]{3,1,2,0:T(8,128)} copy(f32[2,36,12,132]{1,0,3,2:T(2,128)} %bitcast.58) | data formatting | bytes 912384 | tf_op jit(solution)/shard_map/reshape | solution.py:65
  246.3 1.3 add.441
  (163 shorter events, 36.2 us)
Async XLA Ops:
  1.0 49.3 %copy-start.4 = (f32[32,8,128]{2,0,1:T(8,128)}, f32[32,8,128]{2,0,1:T(8,128)S(1)}, u32[]{:S(2)}) copy-start(f32[32,8,128]{2,0,1:T(8,128)S(1)} %get-tuple-element.23) | copy-start | bytes 393220
  2.1 8.1 %collective-permute-start = (f32[3,32,3,128]{3,1,2,0:T(8,128)S(1)}, f32[3,32,3,128]{3,1,2,0:T(8,128)S(1)}, u32[]{:S(2)}, u32[]{:S(2)}) collective-permute-start(f32[3,32,3,128]{3,1,2,0:T(8,128)S(1)} %get-tuple-element.17), channel_id=1, source_target_pairs={{0,4},{4,8},{8,12},{1,5},{5,9},{9,13},{2,6},{6,10},{10,14},{3,7},{... | collective-permute-start | bytes 442376 | tf_op jit(solution)/shard_map/ppermute | solution.py:24
  7.0 7.2 %collective-permute-start.1 = (f32[3,32,3,128]{3,1,2,0:T(8,128)S(1)}, f32[3,32,3,128]{3,1,2,0:T(8,128)S(1)}, u32[]{:S(2)}, u32[]{:S(2)}) collective-permute-start(f32[3,32,3,128]{3,1,2,0:T(8,128)S(1)} %get-tuple-element.18), channel_id=1, source_target_pairs={{4,0},{8,4},{12,8},{5,1},{9,5},{13,9},{6,2},{10,6},{14,10},{7,3},{... | collective-permute-start | bytes 442376 | tf_op jit(solution)/shard_map/ppermute | solution.py:26
  14.3 16.5 %collective-permute-start.2 = (f32[3,3,14,128]{3,1,2,0:T(4,128)S(1)}, f32[3,3,14,128]{3,1,2,0:T(4,128)S(1)}, u32[]{:S(2)}, u32[]{:S(2)}) collective-permute-start(f32[3,3,14,128]{3,1,2,0:T(4,128)S(1)} %get-tuple-element.11), channel_id=1, source_target_pairs={{0,1},{1,2},{2,3},{4,5},{5,6},{6,7},{8,9},{9,10},{10,11},{12,13},{... | collective-permute-start | bytes 193544 | tf_op jit(solution)/shard_map/ppermute | solution.py:24
  15.6 15.2 %collective-permute-start.3 = (f32[3,3,14,128]{3,1,2,0:T(4,128)S(1)}, f32[3,3,14,128]{3,1,2,0:T(4,128)S(1)}, u32[]{:S(2)}, u32[]{:S(2)}) collective-permute-start(f32[3,3,14,128]{3,1,2,0:T(4,128)S(1)} %get-tuple-element.12), channel_id=1, source_target_pairs={{1,0},{2,1},{3,2},{5,4},{6,5},{7,6},{9,8},{10,9},{11,10},{13,12},{... | collective-permute-start | bytes 193544 | tf_op jit(solution)/shard_map/ppermute | solution.py:26
  33.7 7.0 %collective-permute-start.4 = (f32[3,38,14,3]{1,2,3,0:T(8,128)S(1)}, f32[3,38,14,3]{1,2,3,0:T(8,128)S(1)}, u32[]{:S(2)}, u32[]{:S(2)}) collective-permute-start(f32[3,38,14,3]{1,2,3,0:T(8,128)S(1)} %copy.81), channel_id=1, source_target_pairs={{0,16},{1,17},{2,18},{3,19},{4,20},{5,21},{6,22},{7,23},{8,24},{9,... | collective-permute-start | bytes 57464 | tf_op jit(solution)/shard_map/ppermute | solution.py:24
  37.6 6.2 %collective-permute-start.5 = (f32[3,38,14,3]{1,2,3,0:T(8,128)S(1)}, f32[3,38,14,3]{1,2,3,0:T(8,128)S(1)}, u32[]{:S(2)}, u32[]{:S(2)}) collective-permute-start(f32[3,38,14,3]{1,2,3,0:T(8,128)S(1)} %copy.82), channel_id=1, source_target_pairs={{16,0},{17,1},{18,2},{19,3},{20,4},{21,5},{22,6},{23,7},{24,8},{25... | collective-permute-start | bytes 57464 | tf_op jit(solution)/shard_map/ppermute | solution.py:26
  39.5 5.7 %copy-start.17 = (f32[16,4,64]{2,1,0:T(4,128)}, f32[16,4,64]{2,1,0:T(4,128)S(1)}, u32[]{:S(2)}) copy-start(f32[16,4,64]{2,1,0:T(4,128)S(1)} %get-tuple-element.29) | copy-start | bytes 49156
  49.6 1.0 copy-start.2
  69.1 7.1 %copy-start.19 = (f32[1,16,4,64]{3,2,1,0:T(4,128)S(1)}, f32[1,16,4,64]{3,2,1,0:T(4,128)}, u32[]{:S(2)}) copy-start(f32[1,16,4,64]{3,2,1,0:T(4,128)} %get-tuple-element.30) | copy-start | bytes 49156
  76.2 6.2 %collective-permute-start.6 = (f32[3,16,4,64]{3,1,2,0:T(8,128)S(1)}, f32[3,16,4,64]{3,1,2,0:T(8,128)S(1)}, u32[]{:S(2)}, u32[]{:S(2)}) collective-permute-start(f32[3,16,4,64]{3,1,2,0:T(8,128)S(1)} %copy_dynamic-update-slice_fusion.1), channel_id=1, source_target_pairs={{0,4},{4,8},{8,12},{1,5},{5,9},{9,13},{2,6},{6,10},{10,14},{3,7},{... | collective-permute-start | bytes 147464 | tf_op jit(solution)/shard_map/ppermute | solution.py:24
  79.7 7.5 %collective-permute-start.7 = (f32[3,16,4,64]{3,1,2,0:T(8,128)S(1)}, f32[3,16,4,64]{3,1,2,0:T(8,128)}, u32[]{:S(2)}, u32[]{:S(2)}) collective-permute-start(f32[3,16,4,64]{3,1,2,0:T(8,128)S(1)} %copy_dynamic-update-slice_fusion.1), channel_id=1, source_target_pairs={{4,0},{8,4},{12,8},{5,1},{9,5},{13,9},{6,2},{10,6},{14,10},{7,3},{... | collective-permute-start | bytes 147464 | tf_op jit(solution)/shard_map/ppermute | solution.py:26
  88.0 4.8 %collective-permute-start.8 = (f32[3,4,12,64]{3,1,2,0:T(4,128)S(1)}, f32[3,4,12,64]{3,1,2,0:T(4,128)S(1)}, u32[]{:S(2)}, u32[]{:S(2)}) collective-permute-start(f32[3,4,12,64]{3,1,2,0:T(4,128)S(1)} %get-tuple-element.19), channel_id=1, source_target_pairs={{0,1},{1,2},{2,3},{4,5},{5,6},{6,7},{8,9},{9,10},{10,11},{12,13},{... | collective-permute-start | bytes 110600 | tf_op jit(solution)/shard_map/ppermute | solution.py:24
  90.1 6.2 %collective-permute-start.9 = (f32[3,4,12,64]{3,1,2,0:T(4,128)S(1)}, f32[3,4,12,64]{3,1,2,0:T(4,128)S(1)}, u32[]{:S(2)}, u32[]{:S(2)}) collective-permute-start(f32[3,4,12,64]{3,1,2,0:T(4,128)S(1)} %get-tuple-element.20), channel_id=1, source_target_pairs={{1,0},{2,1},{3,2},{5,4},{6,5},{7,6},{9,8},{10,9},{11,10},{13,12},{... | collective-permute-start | bytes 110600 | tf_op jit(solution)/shard_map/ppermute | solution.py:26
  97.5 11.4 %collective-permute-start.10 = (f32[3,24,12,4]{3,1,2,0:T(8,128)S(1)}, f32[3,24,12,4]{3,1,2,0:T(8,128)S(1)}, u32[]{:S(2)}, u32[]{:S(2)}) collective-permute-start(f32[3,24,12,4]{3,1,2,0:T(8,128)S(1)} %get-tuple-element.15), channel_id=1, source_target_pairs={{0,16},{1,17},{2,18},{3,19},{4,20},{5,21},{6,22},{7,23},{8,24},{9,... | collective-permute-start | bytes 41480 | tf_op jit(solution)/shard_map/ppermute | solution.py:24
  100.4 13.2 %collective-permute-start.11 = (f32[3,24,12,4]{3,1,2,0:T(8,128)S(1)}, f32[3,24,12,4]{3,1,2,0:T(8,128)S(1)}, u32[]{:S(2)}, u32[]{:S(2)}) collective-permute-start(f32[3,24,12,4]{3,1,2,0:T(8,128)S(1)} %get-tuple-element.16), channel_id=1, source_target_pairs={{16,0},{17,1},{18,2},{19,3},{20,4},{21,5},{22,6},{23,7},{24,8},{25... | collective-permute-start | bytes 41480 | tf_op jit(solution)/shard_map/ppermute | solution.py:26
  115.5 1.1 copy-start.18
  115.9 0.7 copy-start
  198.6 0.8 copy-start.8
  232.4 0.9 copy-start.9
  234.0 3.0 %copy-start.1 = (f32[2,22,10,70]{3,2,1,0:T(8,128)S(1)}, f32[2,22,10,70]{3,2,1,0:T(8,128)}, u32[]{:S(2)}) copy-start(f32[2,22,10,70]{3,2,1,0:T(8,128)} %copy-done) | copy-start | bytes 369604
  237.0 0.9 copy-start.13
  237.0 0.9 copy-start.14
  237.1 1.0 copy-start.10
  237.2 1.2 copy-start.15
  237.2 1.2 copy-start.16
  237.2 1.2 copy-start.11
  247.9 1.0 copy-start.6
  247.9 1.1 copy-start.7
  250.1 1.0 copy-start.3
  250.1 1.0 copy-start.5
  250.1 1.0 copy-start.12
